TPU v7x, 32 devices: a whole 2x2x4 slice. The times are simulated.
32 devices in a mesh: pts: 8 (over y, x, core), val: 4 (over z).
Axes of the slice: x: 2, y: 2, z: 4, core: 2. Of those that a mesh axis runs over, the one named last changes fastest.
Arguments:
- trials: bfloat16 [2, 1024, 1024], P(None, 'val', 'pts'), may hold values from -6 to 6
- psi_val: bfloat16 [8192, 1024], P('pts', 'val'), may hold values from -0.1875 to 0.1875
- psi_cond: bfloat16 [8192, 1024], P('pts'), may hold values from -0.1875 to 0.1875
- kernel: bfloat16 [8192, 8192], P(None, ('pts', 'val')), may hold values from -0.5 to 0.5
- eps_val: float32 [1024], P('val'), may hold values from -1.75 to -0.25
- eps_cond: float32 [1024], replicated, may hold values from 0.5 to 1.5
Outputs:
- first: float32 [2, 1024, 1024], P(None, 'val', 'pts')
- filtered: float32 [2, 1024, 1024], P(None, 'val', 'pts')
All inputs are finite; a program needn't handle non-finite values.
Results may differ from a plain program's by a relative error of at most 0.025.
Values may be sent and summed in bfloat16 or wider, within the bound.
A program may use at most 64 MiB of HBM per device.

v0:
```python
import jax
import jax.numpy as jnp
from jax import lax
from jax.sharding import PartitionSpec as P

center_shift = 1.75
half_width = 1.25


def gathered_inner(local_trial, psi_cond):
    return jnp.einsum(
        "kvc,mc->kvm",
        lax.all_gather(local_trial, "pts", axis=2, tiled=True),
        psi_cond,
        preferred_element_type=jnp.float32,
    )


def orbital_terms(inner, psi_val, psi_cond, kernel):
    rho_part = jnp.einsum("mv,kvm->km", psi_val.astype(jnp.float32), inner)
    rho = lax.psum_scatter(rho_part, "val", scatter_dimension=1, tiled=True).astype(jnp.bfloat16)
    image_part = jnp.einsum("km,nm->kn", rho, kernel, preferred_element_type=jnp.float32)
    image_rows = lax.psum_scatter(
        image_part.astype(jnp.bfloat16), "pts", scatter_dimension=1, tiled=True
    ).astype(jnp.float32)
    image = lax.psum(image_rows, "val")
    weighted = (jnp.transpose(psi_val.astype(jnp.float32))[None] * image[:, None, :]).astype(
        jnp.bfloat16
    )
    return jnp.einsum("kvm,mc->kvc", weighted, psi_cond, preferred_element_type=jnp.float32)


def reduced(partial_sum):
    return lax.psum_scatter(
        partial_sum.astype(jnp.bfloat16), "pts", scatter_dimension=2, tiled=True
    ).astype(jnp.float32)


def local(trials, psi_val, psi_cond, kernel, eps_val, eps_cond):
    cols_own = trials.shape[2]
    index_pts = lax.axis_index("pts")
    diff_whole = (eps_cond[None, :] - eps_val[:, None] - center_shift)[None]
    diff_own = lax.dynamic_slice_in_dim(diff_whole, index_pts * cols_own, cols_own, 2)
    first_image = reduced(
        orbital_terms(gathered_inner(trials, psi_cond), psi_val, psi_cond, kernel)
    )
    first = (diff_own * trials.astype(jnp.float32) + 2.0 * first_image) / half_width
    second_trial = first.astype(jnp.bfloat16)
    second_inner = gathered_inner(second_trial, psi_cond)
    second_image = reduced(orbital_terms(second_inner, psi_val, psi_cond, kernel))
    filtered = 2.0 * (
        diff_own * second_trial.astype(jnp.float32) + 2.0 * second_image
    ) / half_width - trials.astype(jnp.float32)
    return (first, filtered)


def solution(mesh):
    in_specs = (
        P(None, "val", "pts"),
        P("pts", "val"),
        P("pts", None),
        P(None, ("pts", "val")),
        P("val"),
        P(),
    )
    out_specs = (P(None, "val", "pts"), P(None, "val", "pts"))
    return jax.shard_map(local, mesh=mesh, in_specs=in_specs, out_specs=out_specs, check_vma=False)
```

profile of v0, /device:TPU:0, one launch (start us, length us, event | category | flops | bytes accessed | tf_op | source)
XLA Modules:
  0.0 326.2 jit_solution(14909899464436743166)
XLA Ops:
  7.2 0.0 copy-start
  7.2 0.0 all-gather.3.cloned.1.call-start
  7.2 0.7 all-gather.3.cloned.1.call-update
  7.9 0.0 reduce-scatter.15.cloned.1.call-start
  8.0 28.1 %all-gather.3.cloned.1.call-done = bf16[2,256,1024]{2,1,0:T(8,128)(2,1)} async-done(((bf16[2,256,128]{2,1,0:T(8,128)(2,1)}), bf16[2,256,1024]{2,1,0:T(8,128)(2,1)}) %all-gather.3.cloned.1.call-update) | async-done | bytes 1048592 | tf_op jit(solution)/shard_map/all_gather | solution.py:13
  36.1 0.0 copy-done
  36.1 2.5 fusion.6
  38.6 2.0 copy.10
  40.6 3.4 %fusion.20 = f32[1024,1,2]{2,1,0:T(1,128)} fusion(bf16[2,256,1024]{1,0,2:T(2,128)(2,1)} %copy.10, bf16[1024,256,1]{1,0,2:T(8,128)(2,1)} %bitcast.48), kind=kOutput, calls=%fused_computation.21 | convolution fusion | flops 1048576 | bytes 1581056 | tf_op jit(solution)/shard_map/mv,kvm->km/dot_general | solution.py:20
  44.0 0.0 reduce-scatter.15.cloned.1.call-update
  44.1 0.0 reduce-scatter.19.cloned.1.call-start
  44.1 22.0 %reduce-scatter.15.cloned.1.call-done = f32[2,256]{0,1:T(8,128)} async-done(((f32[2,1024]{0,1:T(8,128)}), f32[2,256]{0,1:T(8,128)}) %reduce-scatter.15.cloned.1.call-update) | async-done | bytes 2064 | tf_op jit(solution)/shard_map/reduce_scatter | solution.py:21
  66.1 3.4 %convolution_convert_fusion.1 = bf16[2,8192]{1,0:T(2,128)(2,1)S(1)} fusion(bf16[8192,256]{1,0:T(8,128)(2,1)} %param.9, f32[2,256]{0,1:T(8,128)} %reduce-scatter.15.cloned.1.call-done), kind=kOutput, calls=%fused_computation.1 | convolution fusion | flops 8405504 | bytes 4229120 | tf_op jit(solution)/shard_map/km,nm->kn/dot_general | solution.py:22
  69.5 1.9 copy.15
  71.4 0.0 reduce-scatter.19.cloned.1.call-update
  71.4 0.0 reduce-scatter.21.cloned.1.call-start
  71.5 1.1 convert_bitcast_fusion
  72.6 1.3 copy.9
  74.0 37.0 %reduce-scatter.19.cloned.1.call-done = bf16[1024,2]{1,0:T(8,128)(2,1)} async-done(((bf16[8192,2]{1,0:T(8,128)(2,1)}), bf16[1024,2]{1,0:T(8,128)(2,1)}) %reduce-scatter.19.cloned.1.call-update) | async-done | bytes 4112
  111.0 1.1 copy.16
  112.0 11.9 %psum.14 = f32[2,1024]{1,0:T(2,128)S(1)} all-reduce(bf16[2,1024]{1,0:T(2,128)(2,1)S(1)} %copy.16), channel_id=1, replica_groups=mesh['pts'=8,'val'=4] {'val'}, use_global_device_ids=true, to_apply=%region_2.0 | all-reduce | flops 2048 | bytes 12288 | tf_op jit(solution)/shard_map/psum | solution.py:26
  124.0 3.4 %fusion.8 = bf16[2,256,1024]{2,1,0:T(8,128)(2,1)} fusion(bf16[1024,1024]{1,0:T(8,128)(2,1)S(1)} %copy-done, f32[2,1024]{1,0:T(2,128)S(1)} %psum.14, f32[256,1024]{1,0:T(8,128)} %copy.9), kind=kOutput, calls=%fused_computation.12 | convolution fusion | flops 1075314688 | bytes 4202496 | tf_op jit(solution)/shard_map/kvm,mc->kvc/dot_general | solution.py:30
  127.4 2.5 copy.17
  129.9 0.0 copy-start.4
  129.9 0.0 copy-start.1
  130.0 1.2 copy.23
  131.2 0.0 reduce-scatter.21.cloned.1.call-update
  131.2 0.0 all-gather.5.cloned.1.call-start
  131.2 0.8 dynamic-slice.4
  132.0 0.0 copy-done.4
  132.0 0.1 subtract_add_fusion
  132.1 32.4 %reduce-scatter.21.cloned.1.call-done = bf16[128,512]{1,0:T(8,128)(2,1)} async-done(((bf16[1024,512]{1,0:T(8,128)(2,1)}), bf16[128,512]{1,0:T(8,128)(2,1)}) %reduce-scatter.21.cloned.1.call-update) | async-done | bytes 131088
  164.5 0.9 reshape.18
  165.5 0.1 copy.18
  165.6 0.0 copy-done.1
  165.6 0.8 fusion.26
  166.4 0.0 all-gather.5.cloned.1.call-update
  166.4 0.0 reduce-scatter.17.cloned.1.call-start
  166.5 23.8 %all-gather.5.cloned.1.call-done = bf16[2,256,1024]{2,1,0:T(8,128)(2,1)} async-done(((bf16[2,256,128]{2,1,0:T(8,128)(2,1)}), bf16[2,256,1024]{2,1,0:T(8,128)(2,1)}) %all-gather.5.cloned.1.call-update) | async-done | bytes 1048592 | tf_op jit(solution)/shard_map/all_gather | solution.py:13
  190.3 2.5 fusion.2
  192.9 2.0 copy.13
  194.9 3.4 %fusion.18 = f32[1024,1,2]{2,1,0:T(1,128)} fusion(bf16[2,256,1024]{1,0,2:T(2,128)(2,1)} %copy.13, bf16[1024,256,1]{1,0,2:T(8,128)(2,1)} %bitcast.49), kind=kOutput, calls=%fused_computation.19 | convolution fusion | flops 1048576 | bytes 1581056 | tf_op jit(solution)/shard_map/mv,kvm->km/dot_general | solution.py:20
  198.3 0.0 reduce-scatter.17.cloned.1.call-update
  198.3 0.0 reduce-scatter.23.cloned.1.call-start
  198.3 22.0 %reduce-scatter.17.cloned.1.call-done = f32[2,256]{0,1:T(8,128)} async-done(((f32[2,1024]{0,1:T(8,128)}), f32[2,256]{0,1:T(8,128)}) %reduce-scatter.17.cloned.1.call-update) | async-done | bytes 2064 | tf_op jit(solution)/shard_map/reduce_scatter | solution.py:21
  220.3 3.4 %convolution_convert_fusion = bf16[2,8192]{1,0:T(2,128)(2,1)S(1)} fusion(bf16[8192,256]{1,0:T(8,128)(2,1)} %param.9, f32[2,256]{0,1:T(8,128)} %reduce-scatter.17.cloned.1.call-done), kind=kOutput, calls=%fused_computation | convolution fusion | flops 8405504 | bytes 4229120 | tf_op jit(solution)/shard_map/km,nm->kn/dot_general | solution.py:22
  223.7 0.0 copy-start.3
  223.7 1.9 copy.19
  225.7 0.0 reduce-scatter.23.cloned.1.call-update
  225.7 0.0 reduce-scatter.25.cloned.1.call-start
  225.7 39.5 %reduce-scatter.23.cloned.1.call-done = bf16[1024,2]{1,0:T(8,128)(2,1)} async-done(((bf16[8192,2]{1,0:T(8,128)(2,1)}), bf16[1024,2]{1,0:T(8,128)(2,1)}) %reduce-scatter.23.cloned.1.call-update) | async-done | bytes 4112
  265.2 1.1 copy.20
  266.3 11.9 %psum.15 = f32[2,1024]{1,0:T(2,128)S(1)} all-reduce(bf16[2,1024]{1,0:T(2,128)(2,1)S(1)} %copy.20), channel_id=1, replica_groups=mesh['pts'=8,'val'=4] {'val'}, use_global_device_ids=true, to_apply=%region_6.0 | all-reduce | flops 2048 | bytes 12288 | tf_op jit(solution)/shard_map/psum | solution.py:26
  278.2 0.0 copy-done.3
  278.2 2.2 fusion.11
  280.4 2.5 copy.21
  283.0 0.0 copy-start.2
  283.0 1.2 copy.24
  284.2 0.0 reduce-scatter.25.cloned.1.call-update
  284.2 33.3 %reduce-scatter.25.cloned.1.call-done = bf16[128,512]{1,0:T(8,128)(2,1)} async-done(((bf16[1024,512]{1,0:T(8,128)(2,1)}), bf16[128,512]{1,0:T(8,128)(2,1)}) %reduce-scatter.25.cloned.1.call-update) | async-done | bytes 131088
  317.5 0.9 reshape.22
  318.5 0.1 copy.22
  318.6 0.0 copy-done.2
  318.6 0.8 convert_subtract_fusion
Async XLA Ops:
  7.2 28.9 %copy-start = (bf16[1024,1024]{1,0:T(8,128)(2,1)S(1)}, bf16[1024,1024]{1,0:T(8,128)(2,1)}, u32[]{:S(2)}) copy-start(bf16[1024,1024]{1,0:T(8,128)(2,1)} %param.8) | copy-start | bytes 6291460
  7.2 28.9 %all-gather.3.cloned.1.call-start = ((), (), s32[]{:S(2)}) async-start(), calls=%async_computation.6 | async-start | bytes 1179648 | tf_op jit(solution)/shard_map/all_gather | solution.py:13
  7.9 58.2 %reduce-scatter.15.cloned.1.call-start = ((), (), s32[]{:S(2)}) async-start(), calls=%async_computation.7 | async-start | bytes 655360 | tf_op jit(solution)/shard_map/reduce_scatter | solution.py:21
  44.1 66.9 %reduce-scatter.19.cloned.1.call-start = ((), (), s32[]{:S(2)}) async-start(), calls=%async_computation.10 | async-start | bytes 2359296
  71.4 93.1 %reduce-scatter.21.cloned.1.call-start = ((), (), s32[]{:S(2)}) async-start(), calls=%async_computation.11 | async-start | bytes 1179648
  129.9 2.1 copy-start.4
  129.9 35.7 %copy-start.1 = (bf16[2,256,128]{2,1,0:T(8,128)(2,1)S(1)}, bf16[2,256,128]{2,1,0:T(8,128)(2,1)}, u32[]{:S(2)}) copy-start(bf16[2,256,128]{2,1,0:T(8,128)(2,1)} %param.6) | copy-start | bytes 393220
  131.2 59.2 %all-gather.5.cloned.1.call-start = ((), (), s32[]{:S(2)}) async-start(), calls=%async_computation.8 | async-start | bytes 1179648 | tf_op jit(solution)/shard_map/all_gather | solution.py:13
  166.4 53.9 %reduce-scatter.17.cloned.1.call-start = ((), (), s32[]{:S(2)}) async-start(), calls=%async_computation.9 | async-start | bytes 655360 | tf_op jit(solution)/shard_map/reduce_scatter | solution.py:21
  198.3 66.9 %reduce-scatter.23.cloned.1.call-start = ((), (), s32[]{:S(2)}) async-start(), calls=%async_computation.12 | async-start | bytes 2359296
  223.7 54.5 %copy-start.3 = (f32[256,1024]{1,0:T(8,128)S(1)}, f32[256,1024]{1,0:T(8,128)}, u32[]{:S(2)}) copy-start(f32[256,1024]{1,0:T(8,128)} %copy.9) | copy-start | bytes 3145732
  225.7 91.9 %reduce-scatter.25.cloned.1.call-start = ((), (), s32[]{:S(2)}) async-start(), calls=%async_computation.13 | async-start | bytes 1179648
  283.0 35.7 %copy-start.2 = (bf16[2,256,128]{2,1,0:T(8,128)(2,1)S(1)}, bf16[2,256,128]{2,1,0:T(8,128)(2,1)}, u32[]{:S(2)}) copy-start(bf16[2,256,128]{2,1,0:T(8,128)(2,1)} %get-tuple-element.2) | copy-start | bytes 393220
Sparse Core Ops, SparseCore 0:
  9.9 26.1 all-gather.2
  44.2 21.8 reduce-scatter.14
  71.6 39.3 reduce-scatter.18
  131.3 33.1 reduce-scatter.20
  166.8 23.4 all-gather.4
  198.4 21.8 reduce-scatter.16
  225.8 39.3 reduce-scatter.22
  284.3 33.1 reduce-scatter.24
where the time goes:
time: 327 us; the launch traced here: 326 us
  waiting for transfers between devices  239 us (73%)
  matrix products  24.3 us (7%)
  blocking collectives  23.8 us (7%)
  local copies, waits for them, and re-layouts  21.7 us (7%)
  between operations  14.3 us (4%)
    unnamed x12, waiting for transfers between devices  143 us
    all_gather x2, waiting for transfers between devices, gathered_inner(): lax.all_gather(local_trial, 'pts', axis=2, tiled=True)  52 us
    reduce_scatter x2, waiting for transfers between devices, orbital_terms(): lax.psum_scatter(rho_part, 'val', scatter_dimension=1, tiled=True)  43.9 us
    psum x2, blocking collectives, orbital_terms(): image = lax.psum(image_rows, 'val')  23.8 us
    unnamed x22, local copies, waits for them, and re-layouts  15.6 us
    dot_general x2, matrix products, orbital_terms(): jnp.einsum('km,nm->kn', rho, kernel, preferred_element_type=jnp.float32)  6.88 us
    dot_general x2, matrix products, orbital_terms(): rho_part = jnp.einsum('mv,kvm->km', psi_val.astype(jnp.float32), inner)  6.78 us
  transfers between devices with their start and end apart: 8, of which 8 were waited for; matrix products, arithmetic and copies ran while one was open for 1% of the time, Pallas kernels for 0%

commit v1 on v0

--- a/solution.py
+++ b/solution.py
@@ -1,6 +1,8 @@
 import jax
 import jax.numpy as jnp
 from jax import lax
+from jax.experimental import pallas as pl
+from jax.experimental.pallas import tpu as pltpu
 from jax.sharding import PartitionSpec as P
 
 center_shift = 1.75
@@ -54,7 +56,239 @@
     return (first, filtered)
 
 
+F32, BF16 = jnp.float32, jnp.bfloat16
+SWAP = (0, 2, 1, 3)
+NT = (((1,), (1,)), ((), ()))
+
+
+def fused_kernel(n_pts, n_val, x_ref, pv_hbm, pc_hbm, kern_hbm, ev_ref, ec_ref, first_ref, filt_ref,
+                 pv, pvt, cond, kern, diff, second, xg, rs, rr, im, ir, ws, wr,
+                 acc, part_out, part_in, link_out, link_in, load_sem, send_sem, recv_sem):
+    p = lax.axis_index("pts")
+    z = lax.axis_index("val")
+    core = lax.rem(p, 2)
+    n_k, rows, cols = x_ref.shape
+    pts_own = pv.shape[0]
+    width = rr.shape[3]
+
+    def flipped(q, bit):
+        return q + bit - 2 * bit * lax.rem(lax.div(q, bit), 2)
+
+    bit_a, bit_b = 2 + 2 * core, 4 - 2 * core
+    mate, nbr_a, nbr_b = flipped(p, 1), flipped(p, bit_a), flipped(p, bit_b)
+    places = (p, nbr_a, nbr_b, flipped(nbr_a, bit_b))
+
+    loads = [pltpu.make_async_copy(pv_hbm, pv, load_sem.at[0])]
+    for j in range(4):
+        for h in range(2):
+            owner = places[j] if h == 0 else flipped(places[j], 1)
+            at = pl.multiple_of(owner * cols, cols)
+            loads.append(pltpu.make_async_copy(
+                pc_hbm.at[:, pl.ds(at, cols)], cond.at[j, :, pl.ds(h * cols, cols)], load_sem.at[1 + 2 * j + h]))
+    loads.append(pltpu.make_async_copy(kern_hbm, kern, load_sem.at[9]))
+    for load in loads:
+        load.start()
+
+    barrier = pltpu.get_barrier_semaphore()
+    for r in range(1, n_pts):
+        pl.semaphore_signal(barrier, inc=1, device_id=(lax.rem(p + r, n_pts), z), device_id_type=pl.DeviceIdType.MESH)
+    for s in range(1, n_val):
+        pl.semaphore_signal(barrier, inc=1, device_id=(p, lax.rem(z + s, n_val)), device_id_type=pl.DeviceIdType.MESH)
+    pl.semaphore_wait(barrier, n_pts + n_val - 2)
+
+    sent = []
+
+    def remote(it, n, src, dst, to_p, to_z):
+        copy = pltpu.make_async_remote_copy(
+            src_ref=src, dst_ref=dst, send_sem=send_sem.at[it, n], recv_sem=recv_sem.at[it, n],
+            device_id=(to_p, to_z), device_id_type=pl.DeviceIdType.MESH)
+        copy.start()
+        sent.append(copy)
+        return copy
+
+    def gather_start(it, x):
+        g = {}
+        for k in range(n_k):
+            g["a", k] = remote(it, k, x.at[k], xg.at[it, 1, 0, k], nbr_a, z)
+            g["b", k] = remote(it, 2 + k, x.at[k], xg.at[it, 2, 0, k], nbr_b, z)
+            g["m0", k] = remote(it, 4 + k, x.at[k], xg.at[it, 0, 1, k], mate, z)
+        return g
+
+    def density(it, j, x, rho):
+        wide = cond.shape[1]
+        step = 256
+        left = x[...] if j == 0 else xg[it, j, 0]
+        block = jnp.concatenate([left.reshape(n_k * rows, cols), xg[it, j, 1].reshape(n_k * rows, cols)], axis=1)
+        out = []
+        for t in range(wide // step):
+            zz = lax.dot_general(block, cond[j, t * step:(t + 1) * step, :], NT, preferred_element_type=F32)
+            scale = pvt[:, t * step:(t + 1) * step]
+            for k in range(n_k):
+                y = zz[k * rows:(k + 1) * rows] * scale
+                out.append(jnp.sum(y.reshape(rows // 8, 8, step), axis=0))
+        return out if rho is None else [u + w for u, w in zip(rho, out)]
+
+    def apply(it, x):
+        g = gather_start(it, x)
+        if it == 0:
+            loads[0].wait()
+            pvt[...] = jnp.transpose(pv[...].astype(F32))
+            diff[...] = (ec_ref[:, pl.ds(pl.multiple_of(p * cols, cols), cols)]
+                         - jnp.transpose(jnp.broadcast_to(ev_ref[...], (cols, rows))) - center_shift)
+            for load in loads[1:9]:
+                load.wait()
+        for k in range(n_k):
+            g["a", k].wait_recv()
+            g["d", k] = remote(it, 6 + k, xg.at[it, 1, 0, k], xg.at[it, 3, 0, k], nbr_b, z)
+            g["m2", k] = remote(it, 8 + k, xg.at[it, 1, 0, k], xg.at[it, 2, 1, k], mate, z)
+            g["b", k].wait_recv()
+            g["m1", k] = remote(it, 10 + k, xg.at[it, 2, 0, k], xg.at[it, 1, 1, k], mate, z)
+        for k in range(n_k):
+            g["m0", k].wait_recv()
+        rho = density(it, 0, x, None)
+        for k in range(n_k):
+            g["m1", k].wait_recv()
+        rho = density(it, 1, x, rho)
+        for k in range(n_k):
+            g["d", k].wait_recv()
+            g["m3", k] = remote(it, 12 + k, xg.at[it, 3, 0, k], xg.at[it, 3, 1, k], mate, z)
+        for k in range(n_k):
+            g["m2", k].wait_recv()
+        rho = density(it, 2, x, rho)
+        for k in range(n_k):
+            g["m3", k].wait_recv()
+        rho = density(it, 3, x, rho)
+
+        summed = [jnp.sum(u, axis=0, keepdims=True) for u in rho]
+        rho_part = jnp.concatenate(
+            [jnp.concatenate(summed[k::n_k], axis=1) for k in range(n_k)], axis=0)
+        for s in range(n_val):
+            rs[it, s] = rho_part[:, s * width:(s + 1) * width]
+        got = []
+        for s in range(1, n_val):
+            to = lax.rem(z + s, n_val)
+            got.append(remote(it, 13 + s, rs.at[it, to], rr.at[it, s], p, to))
+        own = rs[it, z]
+        for s in range(1, n_val):
+            got[s - 1].wait_recv()
+            own = own + rr[it, s]
+        own = own.astype(BF16)
+
+        if it == 0:
+            loads[9].wait()
+        for t in range(n_pts):
+            im[it, t] = lax.dot_general(own, kern[t * pts_own:(t + 1) * pts_own, :], NT, preferred_element_type=F32)
+        got = []
+        for r in range(1, n_pts):
+            to = lax.rem(p + r, n_pts)
+            got.append(remote(it, 16 + r, im.at[it, to], ir.at[it, r], to, z))
+        total = im[it, p]
+        for r in range(1, n_pts):
+            got[r - 1].wait_recv()
+            total = total + ir[it, r]
+        ws[it] = total
+        got = [remote(it, 23 + s, ws.at[it], wr.at[it, s], p, lax.rem(z + s, n_val)) for s in range(1, n_val)]
+        for s in range(1, n_val):
+            got[s - 1].wait_recv()
+            total = total + wr[it, s]
+
+        weighted = [(pvt[...] * total[k:k + 1]).astype(BF16) for k in range(n_k)]
+        mated, relayed, from_a, from_b = {}, {}, {}, {}
+        result = [None] * n_k
+
+        def finish(j, k):
+            mated[j, k].wait_recv()
+            value = acc[j, k] + part_in[it, j, k].astype(F32)
+            if j == 3:
+                link_out[it, 0, k] = value.astype(BF16)
+                relayed[k] = remote(it, 35 + k, link_out.at[it, 0, k], link_in.at[it, 0, k], nbr_b, z)
+            elif j == 2:
+                link_out[it, 2, k] = value.astype(BF16)
+                from_b[k] = remote(it, 37 + k, link_out.at[it, 2, k], link_in.at[it, 2, k], nbr_b, z)
+            elif j == 1:
+                relayed[k].wait_recv()
+                link_out[it, 1, k] = (value + link_in[it, 0, k].astype(F32)).astype(BF16)
+                from_a[k] = remote(it, 39 + k, link_out.at[it, 1, k], link_in.at[it, 1, k], nbr_a, z)
+            else:
+                from_b[k].wait_recv()
+                value = value + link_in[it, 2, k].astype(F32)
+                from_a[k].wait_recv()
+                result[k] = value + link_in[it, 1, k].astype(F32)
+
+        order = [(j, k) for j in (3, 2, 1, 0) for k in range(n_k)]
+        for n, (j, k) in enumerate(order):
+            both = jnp.dot(weighted[k], cond[j], preferred_element_type=F32)
+            acc[j, k] = both[:, :cols]
+            part_out[it, j, k] = both[:, cols:].astype(BF16)
+            mated[SWAP[j], k] = remote(it, 27 + 2 * SWAP[j] + k, part_out.at[it, j, k],
+                                       part_in.at[it, SWAP[j], k], mate, z)
+            if n >= 3:
+                finish(*order[n - 3])
+        for n in range(len(order) - 3, len(order)):
+            finish(*order[n])
+        return result
+
+    image = apply(0, x_ref)
+    for k in range(n_k):
+        value = (diff[...] * x_ref[k].astype(F32) + 2.0 * image[k]) / half_width
+        first_ref[k] = value
+        second[k] = value.astype(BF16)
+    image = apply(1, second)
+    for k in range(n_k):
+        filt_ref[k] = 2.0 * (diff[...] * second[k].astype(F32) + 2.0 * image[k]) / half_width - x_ref[k].astype(F32)
+    for copy in sent:
+        copy.wait_send()
+
+
+def fused(n_pts, n_val, trials, psi_val, psi_cond, kernel, eps_val, eps_cond):
+    n_k, rows, cols = trials.shape
+    points = psi_val.shape[0]
+    width = kernel.shape[1]
+    vmem, hbm = pl.BlockSpec(memory_space=pltpu.VMEM), pl.BlockSpec(memory_space=pl.ANY)
+    out = jax.ShapeDtypeStruct((n_k, rows, cols), F32)
+    tile = (n_k, rows, cols)
+    return pl.pallas_call(
+        lambda *refs: fused_kernel(n_pts, n_val, *refs),
+        out_shape=(out, out),
+        in_specs=[vmem, hbm, hbm, hbm, vmem, vmem],
+        out_specs=(vmem, vmem),
+        scratch_shapes=[
+            pltpu.VMEM((points, rows), BF16),
+            pltpu.VMEM((rows, points), F32),
+            pltpu.VMEM((4, points, 2 * cols), BF16),
+            pltpu.VMEM(kernel.shape, BF16),
+            pltpu.VMEM((rows, cols), F32),
+            pltpu.VMEM(tile, BF16),
+            pltpu.VMEM((2, 4, 2) + tile, BF16),
+            pltpu.VMEM((2, n_val, n_k, width), F32),
+            pltpu.VMEM((2, n_val, n_k, width), F32),
+            pltpu.VMEM((2, n_pts, n_k, points), F32),
+            pltpu.VMEM((2, n_pts, n_k, points), F32),
+            pltpu.VMEM((2, n_k, points), F32),
+            pltpu.VMEM((2, n_val, n_k, points), F32),
+            pltpu.VMEM((4,) + tile, F32),
+            pltpu.VMEM((2, 4) + tile, BF16),
+            pltpu.VMEM((2, 4) + tile, BF16),
+            pltpu.VMEM((2, 3) + tile, BF16),
+            pltpu.VMEM((2, 3) + tile, BF16),
+            pltpu.SemaphoreType.DMA((10,)),
+            pltpu.SemaphoreType.DMA((2, 41)),
+            pltpu.SemaphoreType.DMA((2, 41)),
+        ],
+        compiler_params=pltpu.CompilerParams(
+            collective_id=0, has_side_effects=True, vmem_limit_bytes=60 * 1024 * 1024),
+    )(trials, psi_val, psi_cond, kernel, eps_val.reshape(1, -1), eps_cond.reshape(1, -1))
+
+
 def solution(mesh):
+    n_pts, n_val = mesh.shape["pts"], mesh.shape["val"]
+
+    def program(trials, *rest):
+        whole_lanes = trials.shape[2] % 128 == 0 and rest[0].shape[1] % 128 == 0
+        if whole_lanes and trials.shape[0] == 2 and n_pts == 8 and n_val <= 4:
+            return fused(n_pts, n_val, trials, *rest)
+        return local(trials, *rest)
+
     in_specs = (
         P(None, "val", "pts"),
         P("pts", "val"),
@@ -64,4 +298,4 @@
         P(),
     )
     out_specs = (P(None, "val", "pts"), P(None, "val", "pts"))
-    return jax.shard_map(local, mesh=mesh, in_specs=in_specs, out_specs=out_specs, check_vma=False)
+    return jax.shard_map(program, mesh=mesh, in_specs=in_specs, out_specs=out_specs, check_vma=False)

time: 327 us -> 72.6 us (0.22)
  waiting for transfers between devices: 239 us -> 0 us
  Pallas kernels: 0 us -> 68.4 us
  matrix products: 24.3 us -> 0 us
  blocking collectives: 23.8 us -> 0 us
  local copies, waits for them, and re-layouts: 21.7 us -> 3.34 us
  between operations: 14.3 us -> 0.64 us
    unnamed x12 -> x0, waiting for transfers between devices: 143 us -> none
    pallas_call x0 -> x1, Pallas kernels: none -> 68.4 us  [fused(): pl.pallas_call(lambda *refs: fused_kernel(n_pts, n_val, *refs), out_shape...]
    all_gather x2 -> x0, waiting for transfers between devices: 52 us -> none  [gathered_inner(): lax.all_gather(local_trial, 'pts', axis=2, tiled=True)]
    reduce_scatter x2 -> x0, waiting for transfers between devices: 43.9 us -> none  [orbital_terms(): lax.psum_scatter(rho_part, 'val', scatter_dimension=1, tiled=True)]
    dot_general x8 -> x0, matrix products: 24.3 us -> none  [the longest x2 6.88 us: orbital_terms(): jnp.einsum('km,nm->kn', rho, kernel, preferred_element_type=jnp.float32)]
    psum x2 -> x0, blocking collectives: 23.8 us -> none  [orbital_terms(): image = lax.psum(image_rows, 'val')]
    unnamed x22 -> x2, local copies, waits for them, and re-layouts: 15.6 us -> 3.34 us
    dot_general x2 -> x0, local copies, waits for them, and re-layouts: 4.06 us -> none  [gathered_inner(): jnp.einsum('kvc,mc->kvm', lax.all_gather(local_trial, 'pts', axis=2, tile...]
  transfers between devices with their start and end apart: 8 -> 0, of which waited for: 8 -> 0; matrix products, arithmetic and copies ran while one was open for 1% -> 0% of each run, Pallas kernels for 0% -> 0%
where the time goes in v1:
time: 72.6 us; the launch traced here: 72.4 us
  Pallas kernels  68.4 us (94%)
  local copies, waits for them, and re-layouts  3.34 us (5%)
    pallas_call x1, Pallas kernels, fused(): pl.pallas_call(lambda *refs: fused_kernel(n_pts, n_val, *refs), out_shape...  68.4 us
    unnamed x2, local copies, waits for them, and re-layouts  3.34 us

profile of v1, /device:TPU:0, one launch (start us, length us, event | category | flops | bytes accessed | tf_op | source)
XLA Modules:
  0.0 72.4 jit_solution(4587030999200200927)
XLA Ops:
  0.6 68.4 %shard_map.77 = (f32[2,256,128]{2,1,0:T(8,128)}, f32[2,256,128]{2,1,0:T(8,128)}) custom-call(bf16[2,256,128]{2,1,0:T(8,128)(2,1)} %refs_0_.1, bf16[1024,256]{1,0:T(8,128)(2,1)} %refs_1_.1, bf16[1024,1024]{1,0:T(8,128)(2,1)} %refs_2_.1, bf16[8192,256]{1,0:T(8,128)(2,1)} %refs_3_.1, f32[1,256]{1,0:T(1,128)} %bitcast.3, f32[1,1024]{1,0:T(1,128)} %bitcast.2), custom_call_target="tpu_custom_call" | custom-call | tf_op jit(solution)/shard_map/pallas_call | solution.py:250
  69.0 1.7 %copy.10 = f32[2,256,128]{2,1,0:T(8,128)} copy(f32[2,256,128]{2,1,0:T(8,128)} %get-tuple-element.4) | data formatting | bytes 524288
  70.7 1.7 %copy.11 = f32[2,256,128]{2,1,0:T(8,128)} copy(f32[2,256,128]{2,1,0:T(8,128)} %get-tuple-element.5) | data formatting | bytes 524288

commit v2 on v0

--- a/solution.py
+++ b/solution.py
@@ -1,6 +1,8 @@
 import jax
 import jax.numpy as jnp
 from jax import lax
+from jax.experimental import pallas as pl
+from jax.experimental.pallas import tpu as pltpu
 from jax.sharding import PartitionSpec as P
 
 center_shift = 1.75
@@ -54,7 +56,258 @@
     return (first, filtered)
 
 
+F32, BF16 = jnp.float32, jnp.bfloat16
+SWAP = (0, 2, 1, 3)
+NT = (((1,), (1,)), ((), ()))
+
+
+def fused_kernel(n_pts, n_val, x_hbm, pv_hbm, pc_hbm, kern_hbm, ev_ref, ec_ref, first_ref, filt_ref,
+                 x_ref, pv, pvt, cond, kern, diff, second, xg, rs, rr, im, ir, ws, wr,
+                 acc, part_out, part_in, link_out, link_in, load_sem, send_sem, recv_sem):
+    p = lax.axis_index("pts")
+    z = lax.axis_index("val")
+    core = lax.rem(p, 2)
+    n_k, rows, cols = x_ref.shape
+    pts_own = pv.shape[0]
+    width = rr.shape[4]
+    lanes = im.shape[4]
+
+    def flipped(q, bit):
+        return q + bit - 2 * bit * lax.rem(lax.div(q, bit), 2)
+
+    bit_a, bit_b = 2 + 2 * core, 4 - 2 * core
+    mate, nbr_a, nbr_b = flipped(p, 1), flipped(p, bit_a), flipped(p, bit_b)
+    places = (p, nbr_a, nbr_b, flipped(nbr_a, bit_b))
+
+    load_x = pltpu.make_async_copy(x_hbm, x_ref, load_sem.at[10])
+    load_x.start()
+    barrier = pltpu.get_barrier_semaphore()
+    for r in range(1, n_pts):
+        pl.semaphore_signal(barrier, inc=1, device_id=(lax.rem(p + r, n_pts), z), device_id_type=pl.DeviceIdType.MESH)
+    for s in range(1, n_val):
+        pl.semaphore_signal(barrier, inc=1, device_id=(p, lax.rem(z + s, n_val)), device_id_type=pl.DeviceIdType.MESH)
+    loads = [pltpu.make_async_copy(pv_hbm, pv, load_sem.at[0])]
+    for j in range(4):
+        for h in range(2):
+            owner = places[j] if h == 0 else flipped(places[j], 1)
+            at = pl.multiple_of(owner * cols, cols)
+            loads.append(pltpu.make_async_copy(
+                pc_hbm.at[:, pl.ds(at, cols)], cond.at[j, :, pl.ds(h * cols, cols)], load_sem.at[1 + 2 * j + h]))
+    loads.append(pltpu.make_async_copy(kern_hbm, kern, load_sem.at[9]))
+    for load in loads:
+        load.start()
+    load_x.wait()
+    pl.semaphore_wait(barrier, n_pts + n_val - 2)
+
+    sent = []
+    live = {}
+
+    def remote(it, k, n, src, dst, to_p, to_z):
+        copy = pltpu.make_async_remote_copy(
+            src_ref=src, dst_ref=dst, send_sem=send_sem.at[it, k, n], recv_sem=recv_sem.at[it, k, n],
+            device_id=(to_p, to_z), device_id_type=pl.DeviceIdType.MESH)
+        copy.start()
+        sent.append(copy)
+        live[it, k, n] = copy
+
+    def arrived(it, k, n):
+        live[it, k, n].wait_recv()
+
+    def gather_start(it, k, x):
+        remote(it, k, 0, x.at[k], xg.at[it, 1, 0, k], nbr_a, z)
+        remote(it, k, 1, x.at[k], xg.at[it, 2, 0, k], nbr_b, z)
+        remote(it, k, 2, x.at[k], xg.at[it, 0, 1, k], mate, z)
+
+    def gather_relay(it, k):
+        arrived(it, k, 0)
+        remote(it, k, 3, xg.at[it, 1, 0, k], xg.at[it, 3, 0, k], nbr_b, z)
+        remote(it, k, 4, xg.at[it, 1, 0, k], xg.at[it, 2, 1, k], mate, z)
+        arrived(it, k, 1)
+        remote(it, k, 5, xg.at[it, 2, 0, k], xg.at[it, 1, 1, k], mate, z)
+
+    def gather_last(it, k):
+        arrived(it, k, 3)
+        remote(it, k, 6, xg.at[it, 3, 0, k], xg.at[it, 3, 1, k], mate, z)
+
+    def density(it, k, j, left, rho):
+        step = 256
+        arrived(it, k, (2, 5, 4, 6)[j])
+        block = jnp.concatenate([left, xg[it, j, 1, k]], axis=1)
+        out = []
+        for t in range(pts_own // step):
+            zz = lax.dot_general(block, cond[j, t * step:(t + 1) * step, :], NT, preferred_element_type=F32)
+            y = zz * pvt[:, t * step:(t + 1) * step]
+            out.append(jnp.sum(y.reshape(rows // 8, 8, step), axis=0))
+        return out if rho is None else [u + w for u, w in zip(rho, out)]
+
+    def rho_start(it, k, rho):
+        row = jnp.concatenate([jnp.sum(u, axis=0, keepdims=True) for u in rho], axis=1)
+        for s in range(n_val):
+            rs[it, k, s] = row[:, s * width:(s + 1) * width]
+        for s in range(1, n_val):
+            to = lax.rem(z + s, n_val)
+            remote(it, k, 6 + s, rs.at[it, k, to], rr.at[it, k, s], p, to)
+
+    def tiled(row):
+        return jnp.concatenate([row[:, i * lanes:(i + 1) * lanes] for i in range(pts_own // lanes)], axis=0)
+
+    def image_start(it, k):
+        own = rs[it, k, z]
+        for s in range(1, n_val):
+            arrived(it, k, 6 + s)
+            own = own + rr[it, k, s]
+        own = jnp.broadcast_to(own, (8, width)).astype(BF16)
+        if it == 0 and k == 0:
+            loads[9].wait()
+        for t in range(n_pts):
+            part = lax.dot_general(own, kern[t * pts_own:(t + 1) * pts_own, :], NT, preferred_element_type=F32)
+            im[it, k, t] = tiled(part[:1])
+        for r in range(1, n_pts):
+            to = lax.rem(p + r, n_pts)
+            remote(it, k, 9 + r, im.at[it, k, to], ir.at[it, k, r], to, z)
+
+    def image_sum(it, k):
+        total = im[it, k, p]
+        for r in range(1, n_pts):
+            arrived(it, k, 9 + r)
+            total = total + ir[it, k, r]
+        ws[it, k] = total
+        for s in range(1, n_val):
+            remote(it, k, 16 + s, ws.at[it, k], wr.at[it, k, s], p, lax.rem(z + s, n_val))
+
+    def pairs_start(it, k):
+        total = ws[it, k]
+        for s in range(1, n_val):
+            arrived(it, k, 16 + s)
+            total = total + wr[it, k, s]
+        row = jnp.concatenate([total[i:i + 1] for i in range(pts_own // lanes)], axis=1)
+        weighted = (pvt[...] * row).astype(BF16)
+        for j in (3, 2, 1, 0):
+            both = jnp.dot(weighted, cond[j], preferred_element_type=F32)
+            part_out[it, j, k] = both[:, cols:].astype(BF16)
+            remote(it, k, 20 + SWAP[j], part_out.at[it, j, k], part_in.at[it, SWAP[j], k], mate, z)
+            acc[j, k] = both[:, :cols]
+
+    def chip_sum(it, k, j):
+        arrived(it, k, 20 + j)
+        return acc[j, k] + part_in[it, j, k].astype(F32)
+
+    def pairs_send(it, k):
+        link_out[it, 0, k] = chip_sum(it, k, 3).astype(BF16)
+        remote(it, k, 24, link_out.at[it, 0, k], link_in.at[it, 0, k], nbr_b, z)
+        link_out[it, 2, k] = chip_sum(it, k, 2).astype(BF16)
+        remote(it, k, 25, link_out.at[it, 2, k], link_in.at[it, 2, k], nbr_b, z)
+
+    def pairs_relay(it, k):
+        value = chip_sum(it, k, 1)
+        arrived(it, k, 24)
+        link_out[it, 1, k] = (value + link_in[it, 0, k].astype(F32)).astype(BF16)
+        remote(it, k, 26, link_out.at[it, 1, k], link_in.at[it, 1, k], nbr_a, z)
+
+    def pairs_end(it, k):
+        value = chip_sum(it, k, 0)
+        arrived(it, k, 25)
+        value = value + link_in[it, 2, k].astype(F32)
+        arrived(it, k, 26)
+        return value + link_in[it, 1, k].astype(F32)
+
+    def apply(it, x, use):
+        every = range(n_k)
+        if it == 0:
+            for k in every:
+                gather_start(it, k, x)
+            loads[0].wait()
+            pvt[...] = jnp.transpose(pv[...].astype(F32))
+            diff[...] = (ec_ref[:, pl.ds(pl.multiple_of(p * cols, cols), cols)]
+                         - jnp.transpose(jnp.broadcast_to(ev_ref[...], (cols, rows))) - center_shift)
+            for load in loads[1:9]:
+                load.wait()
+        rho = [None] * n_k
+        for k in every:
+            gather_relay(it, k)
+            rho[k] = density(it, k, 0, x[k], None)
+        for k in every:
+            rho[k] = density(it, k, 1, xg[it, 1, 0, k], rho[k])
+            gather_last(it, k)
+            rho[k] = density(it, k, 2, xg[it, 2, 0, k], rho[k])
+            rho[k] = density(it, k, 3, xg[it, 3, 0, k], rho[k])
+            rho_start(it, k, rho[k])
+        for stage in (image_start, image_sum):
+            for k in every:
+                stage(it, k)
+        for k in every:
+            pairs_start(it, k)
+            pairs_send(it, k)
+        for k in every:
+            pairs_relay(it, k)
+        for k in every:
+            use(k, pairs_end(it, k))
+
+    def to_first(k, image):
+        value = (diff[...] * x_ref[k].astype(F32) + 2.0 * image) / half_width
+        second[k] = value.astype(BF16)
+        gather_start(1, k, second)
+        first_ref[k] = value
+
+    def to_filtered(k, image):
+        filt_ref[k] = 2.0 * (diff[...] * second[k].astype(F32) + 2.0 * image) / half_width - x_ref[k].astype(F32)
+
+    apply(0, x_ref, to_first)
+    apply(1, second, to_filtered)
+    for copy in sent:
+        copy.wait_send()
+
+
+def fused(n_pts, n_val, trials, psi_val, psi_cond, kernel, eps_val, eps_cond):
+    n_k, rows, cols = trials.shape
+    points = psi_val.shape[0]
+    width = kernel.shape[1]
+    vmem, hbm = pl.BlockSpec(memory_space=pltpu.VMEM), pl.BlockSpec(memory_space=pl.ANY)
+    out = jax.ShapeDtypeStruct((n_k, rows, cols), F32)
+    tile = (n_k, rows, cols)
+    return pl.pallas_call(
+        lambda *refs: fused_kernel(n_pts, n_val, *refs),
+        out_shape=(out, out),
+        in_specs=[hbm, hbm, hbm, hbm, vmem, vmem],
+        out_specs=(vmem, vmem),
+        scratch_shapes=[
+            pltpu.VMEM(tile, BF16),
+            pltpu.VMEM((points, rows), BF16),
+            pltpu.VMEM((rows, points), F32),
+            pltpu.VMEM((4, points, 2 * cols), BF16),
+            pltpu.VMEM(kernel.shape, BF16),
+            pltpu.VMEM((rows, cols), F32),
+            pltpu.VMEM(tile, BF16),
+            pltpu.VMEM((2, 4, 2) + tile, BF16),
+            pltpu.VMEM((2, n_k, n_val, 1, width), F32),
+            pltpu.VMEM((2, n_k, n_val, 1, width), F32),
+            pltpu.VMEM((2, n_k, n_pts, points // 128, 128), F32),
+            pltpu.VMEM((2, n_k, n_pts, points // 128, 128), F32),
+            pltpu.VMEM((2, n_k, points // 128, 128), F32),
+            pltpu.VMEM((2, n_k, n_val, points // 128, 128), F32),
+            pltpu.VMEM((4,) + tile, F32),
+            pltpu.VMEM((2, 4) + tile, BF16),
+            pltpu.VMEM((2, 4) + tile, BF16),
+            pltpu.VMEM((2, 3) + tile, BF16),
+            pltpu.VMEM((2, 3) + tile, BF16),
+            pltpu.SemaphoreType.DMA((11,)),
+            pltpu.SemaphoreType.DMA((2, n_k, 27)),
+            pltpu.SemaphoreType.DMA((2, n_k, 27)),
+        ],
+        compiler_params=pltpu.CompilerParams(
+            collective_id=0, has_side_effects=True, vmem_limit_bytes=60 * 1024 * 1024),
+    )(trials, psi_val, psi_cond, kernel, eps_val.reshape(1, -1), eps_cond.reshape(1, -1))
+
+
 def solution(mesh):
+    n_pts, n_val = mesh.shape["pts"], mesh.shape["val"]
+
+    def program(trials, *rest):
+        whole_lanes = trials.shape[2] % 128 == 0 and rest[0].shape[1] % 128 == 0
+        if whole_lanes and trials.shape[0] == 2 and n_pts == 8 and n_val <= 4:
+            return fused(n_pts, n_val, trials, *rest)
+        return local(trials, *rest)
+
     in_specs = (
         P(None, "val", "pts"),
         P("pts", "val"),
@@ -64,4 +317,4 @@
         P(),
     )
     out_specs = (P(None, "val", "pts"), P(None, "val", "pts"))
-    return jax.shard_map(local, mesh=mesh, in_specs=in_specs, out_specs=out_specs, check_vma=False)
+    return jax.shard_map(program, mesh=mesh, in_specs=in_specs, out_specs=out_specs, check_vma=False)

time: 327 us -> 72.1 us (0.22)
  waiting for transfers between devices: 239 us -> 0 us
  Pallas kernels: 0 us -> 67.9 us
  matrix products: 24.3 us -> 0 us
  blocking collectives: 23.8 us -> 0 us
  local copies, waits for them, and re-layouts: 21.7 us -> 3.34 us
  between operations: 14.3 us -> 0.64 us
    unnamed x12 -> x0, waiting for transfers between devices: 143 us -> none
    pallas_call x0 -> x1, Pallas kernels: none -> 67.9 us  [fused(): pl.pallas_call(lambda *refs: fused_kernel(n_pts, n_val, *refs), out_shape...]
    all_gather x2 -> x0, waiting for transfers between devices: 52 us -> none  [gathered_inner(): lax.all_gather(local_trial, 'pts', axis=2, tiled=True)]
    reduce_scatter x2 -> x0, waiting for transfers between devices: 43.9 us -> none  [orbital_terms(): lax.psum_scatter(rho_part, 'val', scatter_dimension=1, tiled=True)]
    dot_general x8 -> x0, matrix products: 24.3 us -> none  [the longest x2 6.88 us: orbital_terms(): jnp.einsum('km,nm->kn', rho, kernel, preferred_element_type=jnp.float32)]
    psum x2 -> x0, blocking collectives: 23.8 us -> none  [orbital_terms(): image = lax.psum(image_rows, 'val')]
    unnamed x22 -> x2, local copies, waits for them, and re-layouts: 15.6 us -> 3.34 us
    dot_general x2 -> x0, local copies, waits for them, and re-layouts: 4.06 us -> none  [gathered_inner(): jnp.einsum('kvc,mc->kvm', lax.all_gather(local_trial, 'pts', axis=2, tile...]
  transfers between devices with their start and end apart: 8 -> 0, of which waited for: 8 -> 0; matrix products, arithmetic and copies ran while one was open for 1% -> 0% of each run, Pallas kernels for 0% -> 0%
where the time goes in v2:
time: 72.1 us; the launch traced here: 71.9 us
  Pallas kernels  67.9 us (94%)
  local copies, waits for them, and re-layouts  3.34 us (5%)
    pallas_call x1, Pallas kernels, fused(): pl.pallas_call(lambda *refs: fused_kernel(n_pts, n_val, *refs), out_shape...  67.9 us
    unnamed x2, local copies, waits for them, and re-layouts  3.34 us

profile of v2, /device:TPU:0, one launch (start us, length us, event | category | flops | bytes accessed | tf_op | source)
XLA Modules:
  0.0 71.9 jit_solution(15452622384701180480)
XLA Ops:
  0.6 67.9 %shard_map.77 = (f32[2,256,128]{2,1,0:T(8,128)}, f32[2,256,128]{2,1,0:T(8,128)}) custom-call(bf16[2,256,128]{2,1,0:T(8,128)(2,1)} %refs_0_.1, bf16[1024,256]{1,0:T(8,128)(2,1)} %refs_1_.1, bf16[1024,1024]{1,0:T(8,128)(2,1)} %refs_2_.1, bf16[8192,256]{1,0:T(8,128)(2,1)} %refs_3_.1, f32[1,256]{1,0:T(1,128)} %bitcast.3, f32[1,1024]{1,0:T(1,128)} %bitcast.2), custom_call_target="tpu_custom_call" | custom-call | tf_op jit(solution)/shard_map/pallas_call | solution.py:268
  68.5 1.7 %copy.10 = f32[2,256,128]{2,1,0:T(8,128)} copy(f32[2,256,128]{2,1,0:T(8,128)} %get-tuple-element.4) | data formatting | bytes 524288
  70.2 1.7 %copy.11 = f32[2,256,128]{2,1,0:T(8,128)} copy(f32[2,256,128]{2,1,0:T(8,128)} %get-tuple-element.5) | data formatting | bytes 524288

commit v3 on v2

--- a/solution.py
+++ b/solution.py
@@ -187,16 +187,18 @@
             part_out[it, j, k] = both[:, cols:].astype(BF16)
             remote(it, k, 20 + SWAP[j], part_out.at[it, j, k], part_in.at[it, SWAP[j], k], mate, z)
             acc[j, k] = both[:, :cols]
+            if j == 1:
+                pairs_send(it, k, 3, 0, 24)
+            elif j == 0:
+                pairs_send(it, k, 2, 2, 25)
 
     def chip_sum(it, k, j):
         arrived(it, k, 20 + j)
         return acc[j, k] + part_in[it, j, k].astype(F32)
 
-    def pairs_send(it, k):
-        link_out[it, 0, k] = chip_sum(it, k, 3).astype(BF16)
-        remote(it, k, 24, link_out.at[it, 0, k], link_in.at[it, 0, k], nbr_b, z)
-        link_out[it, 2, k] = chip_sum(it, k, 2).astype(BF16)
-        remote(it, k, 25, link_out.at[it, 2, k], link_in.at[it, 2, k], nbr_b, z)
+    def pairs_send(it, k, j, slot, n):
+        link_out[it, slot, k] = chip_sum(it, k, j).astype(BF16)
+        remote(it, k, n, link_out.at[it, slot, k], link_in.at[it, slot, k], nbr_b, z)
 
     def pairs_relay(it, k):
         value = chip_sum(it, k, 1)
@@ -237,7 +239,6 @@
                 stage(it, k)
         for k in every:
             pairs_start(it, k)
-            pairs_send(it, k)
         for k in every:
             pairs_relay(it, k)
         for k in every:

time: 72.1 us -> 70.3 us (0.975)
  Pallas kernels: 67.9 us -> 66.1 us
    pallas_call x1, Pallas kernels: 67.9 us -> 66.1 us  [fused(): pl.pallas_call(lambda *refs: fused_kernel(n_pts, n_val, *refs), out_shape...]
where the time goes in v3:
time: 70.3 us; the launch traced here: 70.1 us
  Pallas kernels  66.1 us (94%)
  local copies, waits for them, and re-layouts  3.34 us (5%)
    pallas_call x1, Pallas kernels, fused(): pl.pallas_call(lambda *refs: fused_kernel(n_pts, n_val, *refs), out_shape...  66.1 us
    unnamed x2, local copies, waits for them, and re-layouts  3.34 us

profile of v3, /device:TPU:0, one launch (start us, length us, event | category | flops | bytes accessed | tf_op | source)
XLA Modules:
  0.0 70.1 jit_solution(3688204466575039551)
XLA Ops:
  0.6 66.1 %shard_map.77 = (f32[2,256,128]{2,1,0:T(8,128)}, f32[2,256,128]{2,1,0:T(8,128)}) custom-call(bf16[2,256,128]{2,1,0:T(8,128)(2,1)} %refs_0_.1, bf16[1024,256]{1,0:T(8,128)(2,1)} %refs_1_.1, bf16[1024,1024]{1,0:T(8,128)(2,1)} %refs_2_.1, bf16[8192,256]{1,0:T(8,128)(2,1)} %refs_3_.1, f32[1,256]{1,0:T(1,128)} %bitcast.3, f32[1,1024]{1,0:T(1,128)} %bitcast.2), custom_call_target="tpu_custom_call" | custom-call | tf_op jit(solution)/shard_map/pallas_call | solution.py:269
  66.8 1.7 %copy.10 = f32[2,256,128]{2,1,0:T(8,128)} copy(f32[2,256,128]{2,1,0:T(8,128)} %get-tuple-element.4) | data formatting | bytes 524288
  68.4 1.7 %copy.11 = f32[2,256,128]{2,1,0:T(8,128)} copy(f32[2,256,128]{2,1,0:T(8,128)} %get-tuple-element.5) | data formatting | bytes 524288
